TPU v7x, 128 devices: a whole 4x4x4 slice. The times are simulated.
128 devices in a mesh: own: 16 (over y, z), red: 8 (over x, core).
Axes of the slice: x: 4, y: 4, z: 4, core: 2. Of those that a mesh axis runs over, the one named last changes fastest.
Arguments:
- amp_tiles: bfloat16 [8192, 128, 128], P(('own', 'red')), may hold values from -6 to 6
- int_tiles: bfloat16 [8192, 128, 128], P(('own', 'red')), may hold values from -0.0625 to 0.0625
- requests: int32 [16, 8, 16, 2, 8], P('own', 'red'), may hold values from -1 to 63, as said below
- tri_amp: int32 [512, 8, 64], P('own', 'red'), may hold values from 0 to 127, as said below
- tri_int: int32 [512, 8, 64], P('own', 'red'), may hold values from 0 to 127, as said below
- tri_count: int32 [512, 8], P('own', 'red'), may hold values from 1 to 64, as said below
Outputs:
- residual: float32 [512, 128, 128], P(('own', 'red'))
Inputs may be any that keep to these rules, and one draw needn't show every extreme that they name: -1 marks an empty slot and live slots come first; the live numbers in one row of 8 slots are distinct; every owner device has 8 live amplitude requests to some holder and 8 live integral requests to some holder. tri_amp[t, r, k] // 8 is a holder h and tri_amp[t, r, k] % 8 is below the number of live amplitude requests of the owner of t, on red index r, to h. `tri_int`: likewise for the integral requests. `tri_count`: on every owner and red index some residual tile has 64 live triples.
All inputs are finite; a program needn't handle non-finite values.
Results may differ from a plain program's by a relative error of at most 0.0003.
Values may be sent and summed in bfloat16 or wider, within the bound.
No kernel may reach another device: no remote copies, remote signals or barrier semaphores. Data moves between devices by JAX's collectives and lax.ppermute only.
A program may use at most 128 MiB of HBM per device.

v0:
```python
import math
import jax
import jax.numpy as jnp
from jax import lax
from jax.sharding import PartitionSpec as P


def select_tiles(store, wanted):
    clipped = jnp.clip(wanted, 0, store.shape[0] - 1)
    picked = store[clipped]
    return jnp.where((wanted >= 0)[:, :, None, None], picked, jnp.zeros((), store.dtype))


def contract_rows(got_amp, got_int, amp_pos, int_pos, counts):
    row_count, slot_count = amp_pos.shape
    received = got_amp.shape[0]
    tile_width = got_amp.shape[-1]
    block_rows = math.gcd(8, row_count)
    keep_mask = lax.broadcasted_iota(jnp.int32, (row_count, slot_count), 1) < counts[:, None]
    flat_amp = got_amp.reshape(received, tile_width * tile_width)
    flat_int = got_int.reshape(received, tile_width * tile_width)
    slot_iota = lax.broadcasted_iota(jnp.int32, (1, 1, received), 2)

    def one_block(operands):
        block_amp, block_int, block_keep = operands
        pick_amp = ((block_amp[:, :, None] == slot_iota) & block_keep[:, :, None]).astype(
            got_amp.dtype
        )
        pick_int = (block_int[:, :, None] == slot_iota).astype(got_int.dtype)
        left_tiles = jnp.einsum(
            "nkm,mx->nkx", pick_amp, flat_amp, preferred_element_type=jnp.float32
        ).astype(got_amp.dtype)
        right_tiles = jnp.einsum(
            "nkm,mx->nkx", pick_int, flat_int, preferred_element_type=jnp.float32
        ).astype(got_int.dtype)
        left_tiles = left_tiles.reshape(block_rows, slot_count, tile_width, tile_width)
        right_tiles = right_tiles.reshape(block_rows, slot_count, tile_width, tile_width)
        return jnp.einsum(
            "nkpc,nkqc->npq", left_tiles, right_tiles, preferred_element_type=jnp.float32
        )

    def in_blocks(values):
        return values.reshape((row_count // block_rows, block_rows) + values.shape[1:])

    product = lax.map(one_block, (in_blocks(amp_pos), in_blocks(int_pos), in_blocks(keep_mask)))
    return product.reshape(row_count, tile_width, tile_width)


def body(amp_tiles, int_tiles, requests, tri_amp, tri_int, tri_count):
    wanted = requests[0, 0]
    asked = lax.all_to_all(wanted, "own", split_axis=0, concat_axis=0, tiled=True)
    send_amp = select_tiles(amp_tiles, asked[:, 0])
    send_int = select_tiles(int_tiles, asked[:, 1])
    got_amp, got_int = (
        lax.all_to_all(send_amp, "own", split_axis=0, concat_axis=0, tiled=True),
        lax.all_to_all(send_int, "own", split_axis=0, concat_axis=0, tiled=True),
    )
    flat_amp = got_amp.reshape((-1,) + got_amp.shape[2:])
    flat_int = got_int.reshape((-1,) + got_int.shape[2:])
    amp_pos = tri_amp[:, 0]
    int_pos = tri_int[:, 0]
    counts = tri_count[:, 0]
    share = amp_pos.shape[0] // lax.axis_size("red")
    partial_sum = contract_rows(flat_amp, flat_int, amp_pos, int_pos, counts)
    total_sum = lax.psum(partial_sum, "red")
    return lax.dynamic_slice_in_dim(total_sum, lax.axis_index("red") * share, share, 0)


def solution(mesh):
    placed = (
        P(("own", "red"), None, None),
        P(("own", "red"), None, None),
        P("own", "red", None, None, None),
        P("own", "red", None),
        P("own", "red", None),
        P("own", "red"),
    )
    return jax.shard_map(
        body, mesh=mesh, in_specs=placed, out_specs=P(("own", "red"), None, None), check_vma=False
    )
```

profile of v0, /device:TPU:0, one launch (start us, length us, event | category | flops | bytes accessed | tf_op | source)
XLA Modules:
  0.0 401.2 jit_solution(17868745536821819180)
XLA Ops:
  6.5 0.0 copy-start
  6.5 0.9 copy.19
  7.5 15.6 %all_to_all.15 = s32[16,2,8]{2,1,0:T(2,128)S(1)} all-to-all(s32[16,2,8]{2,1,0:T(2,128)S(1)} %bitcast.88), channel_id=1, replica_groups=mesh['own'=16,'red'=8] {'own'}, dimensions={0} | all-to-all | bytes 2048 | tf_op jit(solution)/shard_map/all_to_all | solution.py:51
  23.0 0.1 copy.30
  23.1 0.1 copy.26
  23.2 0.1 reshape.93
  23.3 0.1 copy.25
  23.4 0.0 copy-done
  23.4 3.0 gather_fusion.1
  26.4 6.9 %copy_select_fusion = bf16[16,8,128,128]{3,1,2,0:T(8,128)(2,1)} fusion(bf16[16,8,128,128]{3,2,1,0:T(8,128)(2,1)} %bitcast.85, pred[16,8]{1,0:T(8,128)(4,1)S(1)} %copy.25), kind=kLoop, calls=%fused_computation.21 | loop fusion | flops 2097152 | bytes 8388736 | tf_op jit(solution)/shard_map/jit(_where)/select_n | solution.py:11
  33.3 0.0 copy-start.2
  33.3 4.7 %all-to-all-start.2 = ((bf16[16,8,128,128]{3,1,2,0:T(8,128)(2,1)}), bf16[16,8,128,128]{3,1,2,0:T(8,128)(2,1)}, u32[]{:S(2)}, u32[]{:S(2)}) async-start(bf16[16,8,128,128]{3,1,2,0:T(8,128)(2,1)} %copy_select_fusion), calls=%async_computation.2 | async-start | bytes 8388608 | tf_op jit(solution)/shard_map/all_to_all | solution.py:56
  37.9 0.1 copy.29
  38.0 0.1 copy.22
  38.1 0.1 reshape.85
  38.2 0.1 copy.21
  38.3 0.0 copy-done.2
  38.3 3.0 gather_fusion
  41.3 6.8 %copy_select_fusion.1 = bf16[16,8,128,128]{3,1,2,0:T(8,128)(2,1)} fusion(bf16[16,8,128,128]{3,2,1,0:T(8,128)(2,1)} %bitcast.86, pred[16,8]{1,0:T(8,128)(4,1)S(1)} %copy.21), kind=kLoop, calls=%fused_computation.22 | loop fusion | flops 2097152 | bytes 8388736 | tf_op jit(solution)/shard_map/jit(_where)/select_n | solution.py:11
  48.2 0.0 copy-start.3
  48.2 44.4 %all-to-all-done.2 = bf16[16,8,128,128]{3,1,2,0:T(8,128)(2,1)} async-done(((bf16[16,8,128,128]{3,1,2,0:T(8,128)(2,1)}), bf16[16,8,128,128]{3,1,2,0:T(8,128)(2,1)}, u32[]{:S(2)}, u32[]{:S(2)}) %all-to-all-start.2) | async-done | bytes 4194336 | tf_op jit(solution)/shard_map/all_to_all | solution.py:56
  92.6 5.1 %all-to-all-start.1 = ((bf16[16,8,128,128]{3,1,2,0:T(8,128)(2,1)}), bf16[16,8,128,128]{3,1,2,0:T(8,128)(2,1)}, u32[]{:S(2)}, u32[]{:S(2)}) async-start(bf16[16,8,128,128]{3,1,2,0:T(8,128)(2,1)} %copy_select_fusion.1), calls=%async_computation.1 | async-start | bytes 8388608 | tf_op jit(solution)/shard_map/all_to_all | solution.py:55
  97.7 0.2 all-reduce.2.cloned.1.call-start
  97.9 0.5 broadcast.105
  98.4 0.0 copy-done.3
  98.4 0.6 reduce.3
  99.1 0.1 lt.37
  99.2 0.1 iota_compare_fusion.3
  99.2 48.2 %all-to-all-done.1 = bf16[16,8,128,128]{3,1,2,0:T(8,128)(2,1)} async-done(((bf16[16,8,128,128]{3,1,2,0:T(8,128)(2,1)}), bf16[16,8,128,128]{3,1,2,0:T(8,128)(2,1)}, u32[]{:S(2)}, u32[]{:S(2)}) %all-to-all-start.1) | async-done | bytes 4194336 | tf_op jit(solution)/shard_map/all_to_all | solution.py:55
  147.4 178.1 %while.12 = (s32[]{:T(128)}, f32[4,8,128,128]{3,2,1,0:T(8,128)}, s32[4,8,64]{2,1,0:T(8,128)}, pred[4,8,64]{2,1,0:T(8,128)(4,1)S(1)}, bf16[128,16384]{1,0:T(8,128...) while((s32[]{:T(128)}, f32[4,8,128,128]{3,2,1,0:T(8,128)}, ...), condition=%wide.region_1.2_spmd.clone.clone, body=%wide.region_0.1_spmd.clone.clone.sunk | while | flops 6459424768 | bytes 143145056 | solution.py:45
  147.4 0.7 dynamic-slice_bitcast_fusion.5
  148.1 7.0 %convolution_convert_fusion.5 = bf16[8,64,16384]{2,1,0:T(8,128)(2,1)S(1)} fusion(bf16[128,16384]{1,0:T(8,128)(2,1)} %get-tuple-element.172, s32[8,64]{1,0:T(8,128)S(1)} %get-tuple-element.151, pred[8,64]{1,0:T(8,128)(4,1)S(1)} %dynamic-slice_bitcast_fusion.6), kind=kOutput, calls=%fused_computation.4.clone.1 | convolution fusion | flops 2156003328 | bytes 20974080 | tf_op jit(solution)/shard_map/while/body/eval_jaxpr/nkm,mx->nkx/dot_general | solution.py:30
  155.1 8.3 %copy.38 = bf16[64,8,128,128]{3,2,1,0:T(8,128)(2,1)} copy(bf16[64,8,128,128]{3,1,2,0:T(8,128)(2,1)S(1)} %bitcast.81) | data formatting | bytes 33554432 | tf_op jit(solution)/shard_map/while
  163.4 6.9 %convolution_convert_fusion.4 = bf16[8,64,16384]{2,1,0:T(8,128)(2,1)S(1)} fusion(bf16[128,16384]{1,0:T(8,128)(2,1)} %get-tuple-element.174, s32[8,64]{1,0:T(8,128)S(1)} %get-tuple-element.150), kind=kOutput, calls=%fused_computation.3.clone.1 | convolution fusion | flops 2155937792 | bytes 20973568 | tf_op jit(solution)/shard_map/while/body/eval_jaxpr/nkm,mx->nkx/dot_general | solution.py:33
  170.3 8.3 %copy.37 = bf16[64,8,128,128]{3,2,1,0:T(8,128)(2,1)} copy(bf16[64,8,128,128]{3,1,2,0:T(8,128)(2,1)S(1)} %bitcast.82) | data formatting | bytes 33554432 | tf_op jit(solution)/shard_map/while
  178.6 13.3 %fusion.30 = f32[4,8,128,128]{3,2,1,0:T(8,128)} fusion(f32[4,8,128,128]{3,2,1,0:T(8,128)} %get-tuple-element.161, s32[]{:T(128)} %get-tuple-element.160, bf16[8,64,128,128]{3,2,1,0:T(8,128)(2,1)} %bitcast.84, bf16[8,64,128,128]{3,2,1,0:T(8,128)(2,1)} %bitcast.83), kind=kOutput, calls=%fused_computation.11.clone.1 | convolution fusion | flops 2147483648 | bytes 34079232 | tf_op jit(solution)/shard_map/while/body/eval_jaxpr/nkpc,nkqc->npq/dot_general | solution.py:38
  191.9 0.7 dynamic-slice_bitcast_fusion.5
  192.6 7.0 %convolution_convert_fusion.5 = bf16[8,64,16384]{2,1,0:T(8,128)(2,1)S(1)} fusion(bf16[128,16384]{1,0:T(8,128)(2,1)} %get-tuple-element.172, s32[8,64]{1,0:T(8,128)S(1)} %get-tuple-element.151, pred[8,64]{1,0:T(8,128)(4,1)S(1)} %dynamic-slice_bitcast_fusion.6), kind=kOutput, calls=%fused_computation.4.clone.1 | convolution fusion | flops 2156003328 | bytes 20974080 | tf_op jit(solution)/shard_map/while/body/eval_jaxpr/nkm,mx->nkx/dot_general | solution.py:30
  199.6 8.3 %copy.38 = bf16[64,8,128,128]{3,2,1,0:T(8,128)(2,1)} copy(bf16[64,8,128,128]{3,1,2,0:T(8,128)(2,1)S(1)} %bitcast.81) | data formatting | bytes 33554432 | tf_op jit(solution)/shard_map/while
  207.9 6.9 %convolution_convert_fusion.4 = bf16[8,64,16384]{2,1,0:T(8,128)(2,1)S(1)} fusion(bf16[128,16384]{1,0:T(8,128)(2,1)} %get-tuple-element.174, s32[8,64]{1,0:T(8,128)S(1)} %get-tuple-element.150), kind=kOutput, calls=%fused_computation.3.clone.1 | convolution fusion | flops 2155937792 | bytes 20973568 | tf_op jit(solution)/shard_map/while/body/eval_jaxpr/nkm,mx->nkx/dot_general | solution.py:33
  214.8 8.3 %copy.37 = bf16[64,8,128,128]{3,2,1,0:T(8,128)(2,1)} copy(bf16[64,8,128,128]{3,1,2,0:T(8,128)(2,1)S(1)} %bitcast.82) | data formatting | bytes 33554432 | tf_op jit(solution)/shard_map/while
  223.1 13.3 %fusion.30 = f32[4,8,128,128]{3,2,1,0:T(8,128)} fusion(f32[4,8,128,128]{3,2,1,0:T(8,128)} %get-tuple-element.161, s32[]{:T(128)} %get-tuple-element.160, bf16[8,64,128,128]{3,2,1,0:T(8,128)(2,1)} %bitcast.84, bf16[8,64,128,128]{3,2,1,0:T(8,128)(2,1)} %bitcast.83), kind=kOutput, calls=%fused_computation.11.clone.1 | convolution fusion | flops 2147483648 | bytes 34079232 | tf_op jit(solution)/shard_map/while/body/eval_jaxpr/nkpc,nkqc->npq/dot_general | solution.py:38
  236.4 0.7 dynamic-slice_bitcast_fusion.5
  237.2 7.0 %convolution_convert_fusion.5 = bf16[8,64,16384]{2,1,0:T(8,128)(2,1)S(1)} fusion(bf16[128,16384]{1,0:T(8,128)(2,1)} %get-tuple-element.172, s32[8,64]{1,0:T(8,128)S(1)} %get-tuple-element.151, pred[8,64]{1,0:T(8,128)(4,1)S(1)} %dynamic-slice_bitcast_fusion.6), kind=kOutput, calls=%fused_computation.4.clone.1 | convolution fusion | flops 2156003328 | bytes 20974080 | tf_op jit(solution)/shard_map/while/body/eval_jaxpr/nkm,mx->nkx/dot_general | solution.py:30
  244.1 8.3 %copy.38 = bf16[64,8,128,128]{3,2,1,0:T(8,128)(2,1)} copy(bf16[64,8,128,128]{3,1,2,0:T(8,128)(2,1)S(1)} %bitcast.81) | data formatting | bytes 33554432 | tf_op jit(solution)/shard_map/while
  252.4 6.9 %convolution_convert_fusion.4 = bf16[8,64,16384]{2,1,0:T(8,128)(2,1)S(1)} fusion(bf16[128,16384]{1,0:T(8,128)(2,1)} %get-tuple-element.174, s32[8,64]{1,0:T(8,128)S(1)} %get-tuple-element.150), kind=kOutput, calls=%fused_computation.3.clone.1 | convolution fusion | flops 2155937792 | bytes 20973568 | tf_op jit(solution)/shard_map/while/body/eval_jaxpr/nkm,mx->nkx/dot_general | solution.py:33
  259.4 8.3 %copy.37 = bf16[64,8,128,128]{3,2,1,0:T(8,128)(2,1)} copy(bf16[64,8,128,128]{3,1,2,0:T(8,128)(2,1)S(1)} %bitcast.82) | data formatting | bytes 33554432 | tf_op jit(solution)/shard_map/while
  267.7 13.3 %fusion.30 = f32[4,8,128,128]{3,2,1,0:T(8,128)} fusion(f32[4,8,128,128]{3,2,1,0:T(8,128)} %get-tuple-element.161, s32[]{:T(128)} %get-tuple-element.160, bf16[8,64,128,128]{3,2,1,0:T(8,128)(2,1)} %bitcast.84, bf16[8,64,128,128]{3,2,1,0:T(8,128)(2,1)} %bitcast.83), kind=kOutput, calls=%fused_computation.11.clone.1 | convolution fusion | flops 2147483648 | bytes 34079232 | tf_op jit(solution)/shard_map/while/body/eval_jaxpr/nkpc,nkqc->npq/dot_general | solution.py:38
  281.0 0.7 dynamic-slice_bitcast_fusion.5
  281.7 7.0 %convolution_convert_fusion.5 = bf16[8,64,16384]{2,1,0:T(8,128)(2,1)S(1)} fusion(bf16[128,16384]{1,0:T(8,128)(2,1)} %get-tuple-element.172, s32[8,64]{1,0:T(8,128)S(1)} %get-tuple-element.151, pred[8,64]{1,0:T(8,128)(4,1)S(1)} %dynamic-slice_bitcast_fusion.6), kind=kOutput, calls=%fused_computation.4.clone.1 | convolution fusion | flops 2156003328 | bytes 20974080 | tf_op jit(solution)/shard_map/while/body/eval_jaxpr/nkm,mx->nkx/dot_general | solution.py:30
  288.7 8.3 %copy.38 = bf16[64,8,128,128]{3,2,1,0:T(8,128)(2,1)} copy(bf16[64,8,128,128]{3,1,2,0:T(8,128)(2,1)S(1)} %bitcast.81) | data formatting | bytes 33554432 | tf_op jit(solution)/shard_map/while
  296.9 6.9 %convolution_convert_fusion.4 = bf16[8,64,16384]{2,1,0:T(8,128)(2,1)S(1)} fusion(bf16[128,16384]{1,0:T(8,128)(2,1)} %get-tuple-element.174, s32[8,64]{1,0:T(8,128)S(1)} %get-tuple-element.150), kind=kOutput, calls=%fused_computation.3.clone.1 | convolution fusion | flops 2155937792 | bytes 20973568 | tf_op jit(solution)/shard_map/while/body/eval_jaxpr/nkm,mx->nkx/dot_general | solution.py:33
  303.9 8.3 %copy.37 = bf16[64,8,128,128]{3,2,1,0:T(8,128)(2,1)} copy(bf16[64,8,128,128]{3,1,2,0:T(8,128)(2,1)S(1)} %bitcast.82) | data formatting | bytes 33554432 | tf_op jit(solution)/shard_map/while
  312.2 13.3 %fusion.30 = f32[4,8,128,128]{3,2,1,0:T(8,128)} fusion(f32[4,8,128,128]{3,2,1,0:T(8,128)} %get-tuple-element.161, s32[]{:T(128)} %get-tuple-element.160, bf16[8,64,128,128]{3,2,1,0:T(8,128)(2,1)} %bitcast.84, bf16[8,64,128,128]{3,2,1,0:T(8,128)(2,1)} %bitcast.83), kind=kOutput, calls=%fused_computation.11.clone.1 | convolution fusion | flops 2147483648 | bytes 34079232 | tf_op jit(solution)/shard_map/while/body/eval_jaxpr/nkpc,nkqc->npq/dot_general | solution.py:38
  325.5 0.0 copy-start.1
  325.5 0.0 all-reduce.2.cloned.1.call-update
  325.6 67.1 %all-reduce.2.cloned.1.call-done = f32[32,128,128]{2,1,0:T(8,128)} async-done(((f32[32,128,128]{2,1,0:T(8,128)}), f32[32,128,128]{2,1,0:T(8,128)}) %all-reduce.2.cloned.1.call-update) | async-done | bytes 2097168 | tf_op jit(solution)/shard_map/psum | solution.py:65
  392.7 1.7 constant_dynamic-slice_fusion
  394.3 0.0 copy-done.1
  (12 shorter events, 0.1 us)
Async XLA Ops:
  6.5 16.8 %copy-start = (bf16[64,128,128]{2,1,0:T(8,128)(2,1)S(1)}, bf16[64,128,128]{2,1,0:T(8,128)(2,1)}, u32[]{:S(2)}) copy-start(bf16[64,128,128]{2,1,0:T(8,128)(2,1)} %param.9) | copy-start | bytes 6291460
  33.3 5.0 %copy-start.2 = (bf16[64,128,128]{2,1,0:T(8,128)(2,1)S(1)}, bf16[64,128,128]{2,1,0:T(8,128)(2,1)}, u32[]{:S(2)}) copy-start(bf16[64,128,128]{2,1,0:T(8,128)(2,1)} %param.8) | copy-start | bytes 6291460
  33.3 59.3 %all-to-all-start.2 = ((bf16[16,8,128,128]{3,1,2,0:T(8,128)(2,1)}), bf16[16,8,128,128]{3,1,2,0:T(8,128)(2,1)}, u32[]{:S(2)}, u32[]{:S(2)}) async-start(bf16[16,8,128,128]{3,1,2,0:T(8,128)(2,1)} %copy_select_fusion), calls=%async_computation.2 | async-start | bytes 8388608 | tf_op jit(solution)/shard_map/all_to_all | solution.py:56
  48.2 50.3 %copy-start.3 = (s32[32,1]{0,1:T(1,128)S(1)}, s32[32,1]{0,1:T(1,128)}, u32[]{:S(2)}) copy-start(s32[32,1]{0,1:T(1,128)} %param.13) | copy-start | bytes 388
  92.6 54.8 %all-to-all-start.1 = ((bf16[16,8,128,128]{3,1,2,0:T(8,128)(2,1)}), bf16[16,8,128,128]{3,1,2,0:T(8,128)(2,1)}, u32[]{:S(2)}, u32[]{:S(2)}) async-start(bf16[16,8,128,128]{3,1,2,0:T(8,128)(2,1)} %copy_select_fusion.1), calls=%async_computation.1 | async-start | bytes 8388608 | tf_op jit(solution)/shard_map/all_to_all | solution.py:55
  97.7 295.0 %all-reduce.2.cloned.1.call-start = ((), (), s32[]{:S(2)}) async-start(), calls=%async_computation.3 | async-start | bytes 4194304 | tf_op jit(solution)/shard_map/psum | solution.py:65
  325.5 68.8 %copy-start.1 = (bf16[64,128,128]{2,1,0:T(8,128)(2,1)S(1)}, bf16[64,128,128]{2,1,0:T(8,128)(2,1)}, u32[]{:S(2)}) copy-start(bf16[64,128,128]{2,1,0:T(8,128)(2,1)} %param.9) | copy-start | bytes 6291460
Sparse Core Ops, SparseCore 0:
  325.7 66.9 all-reduce.1
where the time goes:
time: 402 us; the launch traced here: 401 us
  waiting for transfers between devices  160 us (40%)
  matrix products  109 us (27%)
  local copies, waits for them, and re-layouts  79 us (20%)
  blocking collectives  15.6 us (4%)
  other arithmetic  14.4 us (4%)
  between operations  13.5 us (3%)
  starting transfers between devices  9.98 us (2%)
    psum x1, waiting for transfers between devices, body(): total_sum = lax.psum(partial_sum, 'red')  67.1 us
    while x8, local copies, waits for them, and re-layouts  66.3 us
    dot_general x4, matrix products, one_block(): jnp.einsum('nkpc,nkqc->npq', left_tiles, right_tiles, preferred_element_t...  53.3 us
    all_to_all x1, waiting for transfers between devices, body(): lax.all_to_all(send_amp, 'own', split_axis=0, concat_axis=0, tiled=True)  48.2 us
    all_to_all x1, waiting for transfers between devices, body(): lax.all_to_all(send_int, 'own', split_axis=0, concat_axis=0, tiled=True)  44.4 us
    dot_general x4, matrix products, one_block(): jnp.einsum('nkm,mx->nkx', pick_amp, flat_amp, preferred_element_type=jnp....  27.9 us
    dot_general x4, matrix products, one_block(): jnp.einsum('nkm,mx->nkx', pick_int, flat_int, preferred_element_type=jnp....  27.8 us
    all_to_all x1, blocking collectives, body(): lax.all_to_all(wanted, 'own', split_axis=0, concat_axis=0, tiled=True)  15.6 us
  transfers between devices with their start and end apart: 3, of which 3 were waited for; matrix products, arithmetic and copies ran while one was open for 3% of the time, Pallas kernels for 0%

commit v1 on v0

--- a/solution.py
+++ b/solution.py
@@ -62,7 +62,11 @@
     counts = tri_count[:, 0]
     share = amp_pos.shape[0] // lax.axis_size("red")
     partial_sum = contract_rows(flat_amp, flat_int, amp_pos, int_pos, counts)
-    total_sum = lax.psum(partial_sum, "red")
+    size = lax.axis_size("red")
+    total_sum, far = (partial_sum, 1)
+    while far < size:
+        total_sum = total_sum + lax.ppermute(total_sum, "red", [(i, i ^ far) for i in range(size)])
+        far = 2 * far
     return lax.dynamic_slice_in_dim(total_sum, lax.axis_index("red") * share, share, 0)
 
 

time: 402 us -> 426 us (1.060)
  waiting for transfers between devices: 160 us -> 189 us
  between operations: 13.5 us -> 0.08 us
  other arithmetic: 14.4 us -> 19.8 us
  starting transfers between devices: 9.98 us -> 14.4 us
    ppermute x0 -> x3, waiting for transfers between devices: none -> 96.2 us  [body(): lax.ppermute(total_sum, 'red', [(i, i ^ far) for i in range(size)])]
    psum x1 -> x0, waiting for transfers between devices: 67.1 us -> none  [body(): total_sum = lax.psum(partial_sum, 'red')]
    add x0 -> x3, other arithmetic: none -> 5.38 us  [body(): total_sum + lax.ppermute(total_sum, 'red', [(i, i ^ far) for i in range(s...]
    ppermute x0 -> x3, starting transfers between devices: none -> 4.59 us  [body(): lax.ppermute(total_sum, 'red', [(i, i ^ far) for i in range(size)])]
  transfers between devices with their start and end apart: 3 -> 5, of which waited for: 3 -> 5; matrix products, arithmetic and copies ran while one was open for 3% -> 3% of each run, Pallas kernels for 0% -> 0%
where the time goes in v1:
time: 426 us; the launch traced here: 425 us
  waiting for transfers between devices  189 us (44%)
  matrix products  109 us (26%)
  local copies, waits for them, and re-layouts  77.3 us (18%)
  other arithmetic  19.8 us (5%)
  blocking collectives  15.6 us (4%)
  starting transfers between devices  14.4 us (3%)
    ppermute x3, waiting for transfers between devices, body(): lax.ppermute(total_sum, 'red', [(i, i ^ far) for i in range(size)])  96.2 us
    while x8, local copies, waits for them, and re-layouts  66.2 us
    dot_general x4, matrix products, one_block(): jnp.einsum('nkpc,nkqc->npq', left_tiles, right_tiles, preferred_element_t...  53.3 us
    all_to_all x1, waiting for transfers between devices, body(): lax.all_to_all(send_amp, 'own', split_axis=0, concat_axis=0, tiled=True)  48.4 us
    all_to_all x1, waiting for transfers between devices, body(): lax.all_to_all(send_int, 'own', split_axis=0, concat_axis=0, tiled=True)  44.4 us
    dot_general x4, matrix products, one_block(): jnp.einsum('nkm,mx->nkx', pick_amp, flat_amp, preferred_element_type=jnp....  27.9 us
    dot_general x4, matrix products, one_block(): jnp.einsum('nkm,mx->nkx', pick_int, flat_int, preferred_element_type=jnp....  27.8 us
    all_to_all x1, blocking collectives, body(): lax.all_to_all(wanted, 'own', split_axis=0, concat_axis=0, tiled=True)  15.6 us
  transfers between devices with their start and end apart: 5, of which 5 were waited for; matrix products, arithmetic and copies ran while one was open for 3% of the time, Pallas kernels for 0%

profile of v1, /device:TPU:0, one launch (start us, length us, event | category | flops | bytes accessed | tf_op | source)
XLA Modules:
  0.0 425.1 jit_solution(11494110859733789633)
XLA Ops:
  0.0 0.0 copy-start
  0.0 0.9 copy.19
  0.9 15.6 %all_to_all.15 = s32[16,2,8]{2,1,0:T(2,128)S(1)} all-to-all(s32[16,2,8]{2,1,0:T(2,128)S(1)} %bitcast.89), channel_id=1, replica_groups=mesh['own'=16,'red'=8] {'own'}, dimensions={0} | all-to-all | bytes 2048 | tf_op jit(solution)/shard_map/all_to_all | solution.py:51
  16.5 0.1 copy.30
  16.6 0.1 copy.26
  16.7 0.1 reshape.93
  16.8 0.1 copy.25
  16.8 0.0 copy-done
  16.8 3.0 gather_fusion.1
  19.9 6.8 %copy_select_fusion = bf16[16,8,128,128]{3,1,2,0:T(8,128)(2,1)} fusion(bf16[16,8,128,128]{3,2,1,0:T(8,128)(2,1)} %bitcast.86, pred[16,8]{1,0:T(8,128)(4,1)S(1)} %copy.25), kind=kLoop, calls=%fused_computation.21 | loop fusion | flops 2097152 | bytes 8388736 | tf_op jit(solution)/shard_map/jit(_where)/select_n | solution.py:11
  26.7 0.0 copy-start.2
  26.7 4.7 %all-to-all-start.2 = ((bf16[16,8,128,128]{3,1,2,0:T(8,128)(2,1)}), bf16[16,8,128,128]{3,1,2,0:T(8,128)(2,1)}, u32[]{:S(2)}, u32[]{:S(2)}) async-start(bf16[16,8,128,128]{3,1,2,0:T(8,128)(2,1)} %copy_select_fusion), calls=%async_computation.2 | async-start | bytes 8388608 | tf_op jit(solution)/shard_map/all_to_all | solution.py:56
  31.4 0.1 copy.29
  31.5 0.1 copy.22
  31.6 0.1 reshape.85
  31.7 0.1 copy.21
  31.8 0.0 copy-done.2
  31.8 3.0 gather_fusion
  34.8 6.8 %copy_select_fusion.1 = bf16[16,8,128,128]{3,1,2,0:T(8,128)(2,1)} fusion(bf16[16,8,128,128]{3,2,1,0:T(8,128)(2,1)} %bitcast.87, pred[16,8]{1,0:T(8,128)(4,1)S(1)} %copy.21), kind=kLoop, calls=%fused_computation.22 | loop fusion | flops 2097152 | bytes 8388736 | tf_op jit(solution)/shard_map/jit(_where)/select_n | solution.py:11
  41.7 0.0 copy-start.3
  41.7 44.4 %all-to-all-done.2 = bf16[16,8,128,128]{3,1,2,0:T(8,128)(2,1)} async-done(((bf16[16,8,128,128]{3,1,2,0:T(8,128)(2,1)}), bf16[16,8,128,128]{3,1,2,0:T(8,128)(2,1)}, u32[]{:S(2)}, u32[]{:S(2)}) %all-to-all-start.2) | async-done | bytes 4194336 | tf_op jit(solution)/shard_map/all_to_all | solution.py:56
  86.1 5.1 %all-to-all-start.1 = ((bf16[16,8,128,128]{3,1,2,0:T(8,128)(2,1)}), bf16[16,8,128,128]{3,1,2,0:T(8,128)(2,1)}, u32[]{:S(2)}, u32[]{:S(2)}) async-start(bf16[16,8,128,128]{3,1,2,0:T(8,128)(2,1)} %copy_select_fusion.1), calls=%async_computation.1 | async-start | bytes 8388608 | tf_op jit(solution)/shard_map/all_to_all | solution.py:55
  91.2 0.5 broadcast.105
  91.7 0.0 copy-done.3
  91.7 0.6 reduce.3
  92.3 0.1 lt.37
  92.4 0.1 iota_compare_fusion.3
  92.5 48.4 %all-to-all-done.1 = bf16[16,8,128,128]{3,1,2,0:T(8,128)(2,1)} async-done(((bf16[16,8,128,128]{3,1,2,0:T(8,128)(2,1)}), bf16[16,8,128,128]{3,1,2,0:T(8,128)(2,1)}, u32[]{:S(2)}, u32[]{:S(2)}) %all-to-all-start.1) | async-done | bytes 4194336 | tf_op jit(solution)/shard_map/all_to_all | solution.py:55
  140.9 178.0 %while.12 = (s32[]{:T(128)}, f32[4,8,128,128]{3,2,1,0:T(8,128)}, s32[4,8,64]{2,1,0:T(8,128)}, pred[4,8,64]{2,1,0:T(8,128)(4,1)S(1)}, bf16[128,16384]{1,0:T(8,128...) while((s32[]{:T(128)}, f32[4,8,128,128]{3,2,1,0:T(8,128)}, ...), condition=%wide.region_1.2_spmd.clone.clone, body=%wide.region_0.1_spmd.clone.clone.sunk | while | flops 6459424768 | bytes 143145056 | solution.py:45
  140.9 0.7 dynamic-slice_bitcast_fusion.5
  141.6 7.0 %convolution_convert_fusion.5 = bf16[8,64,16384]{2,1,0:T(8,128)(2,1)S(1)} fusion(bf16[128,16384]{1,0:T(8,128)(2,1)} %get-tuple-element.172, s32[8,64]{1,0:T(8,128)S(1)} %get-tuple-element.151, pred[8,64]{1,0:T(8,128)(4,1)S(1)} %dynamic-slice_bitcast_fusion.6), kind=kOutput, calls=%fused_computation.4.clone.1 | convolution fusion | flops 2156003328 | bytes 20974080 | tf_op jit(solution)/shard_map/while/body/eval_jaxpr/nkm,mx->nkx/dot_general | solution.py:30
  148.6 8.3 %copy.38 = bf16[64,8,128,128]{3,2,1,0:T(8,128)(2,1)} copy(bf16[64,8,128,128]{3,1,2,0:T(8,128)(2,1)S(1)} %bitcast.82) | data formatting | bytes 33554432 | tf_op jit(solution)/shard_map/while
  156.8 6.9 %convolution_convert_fusion.4 = bf16[8,64,16384]{2,1,0:T(8,128)(2,1)S(1)} fusion(bf16[128,16384]{1,0:T(8,128)(2,1)} %get-tuple-element.174, s32[8,64]{1,0:T(8,128)S(1)} %get-tuple-element.150), kind=kOutput, calls=%fused_computation.3.clone.1 | convolution fusion | flops 2155937792 | bytes 20973568 | tf_op jit(solution)/shard_map/while/body/eval_jaxpr/nkm,mx->nkx/dot_general | solution.py:33
  163.8 8.3 %copy.37 = bf16[64,8,128,128]{3,2,1,0:T(8,128)(2,1)} copy(bf16[64,8,128,128]{3,1,2,0:T(8,128)(2,1)S(1)} %bitcast.83) | data formatting | bytes 33554432 | tf_op jit(solution)/shard_map/while
  172.1 13.3 %fusion.30 = f32[4,8,128,128]{3,2,1,0:T(8,128)} fusion(f32[4,8,128,128]{3,2,1,0:T(8,128)} %get-tuple-element.161, s32[]{:T(128)} %get-tuple-element.160, bf16[8,64,128,128]{3,2,1,0:T(8,128)(2,1)} %bitcast.85, bf16[8,64,128,128]{3,2,1,0:T(8,128)(2,1)} %bitcast.84), kind=kOutput, calls=%fused_computation.11.clone.1 | convolution fusion | flops 2147483648 | bytes 34079232 | tf_op jit(solution)/shard_map/while/body/eval_jaxpr/nkpc,nkqc->npq/dot_general | solution.py:38
  185.4 0.7 dynamic-slice_bitcast_fusion.5
  186.1 7.0 %convolution_convert_fusion.5 = bf16[8,64,16384]{2,1,0:T(8,128)(2,1)S(1)} fusion(bf16[128,16384]{1,0:T(8,128)(2,1)} %get-tuple-element.172, s32[8,64]{1,0:T(8,128)S(1)} %get-tuple-element.151, pred[8,64]{1,0:T(8,128)(4,1)S(1)} %dynamic-slice_bitcast_fusion.6), kind=kOutput, calls=%fused_computation.4.clone.1 | convolution fusion | flops 2156003328 | bytes 20974080 | tf_op jit(solution)/shard_map/while/body/eval_jaxpr/nkm,mx->nkx/dot_general | solution.py:30
  193.0 8.3 %copy.38 = bf16[64,8,128,128]{3,2,1,0:T(8,128)(2,1)} copy(bf16[64,8,128,128]{3,1,2,0:T(8,128)(2,1)S(1)} %bitcast.82) | data formatting | bytes 33554432 | tf_op jit(solution)/shard_map/while
  201.3 6.9 %convolution_convert_fusion.4 = bf16[8,64,16384]{2,1,0:T(8,128)(2,1)S(1)} fusion(bf16[128,16384]{1,0:T(8,128)(2,1)} %get-tuple-element.174, s32[8,64]{1,0:T(8,128)S(1)} %get-tuple-element.150), kind=kOutput, calls=%fused_computation.3.clone.1 | convolution fusion | flops 2155937792 | bytes 20973568 | tf_op jit(solution)/shard_map/while/body/eval_jaxpr/nkm,mx->nkx/dot_general | solution.py:33
  208.3 8.3 %copy.37 = bf16[64,8,128,128]{3,2,1,0:T(8,128)(2,1)} copy(bf16[64,8,128,128]{3,1,2,0:T(8,128)(2,1)S(1)} %bitcast.83) | data formatting | bytes 33554432 | tf_op jit(solution)/shard_map/while
  216.6 13.3 %fusion.30 = f32[4,8,128,128]{3,2,1,0:T(8,128)} fusion(f32[4,8,128,128]{3,2,1,0:T(8,128)} %get-tuple-element.161, s32[]{:T(128)} %get-tuple-element.160, bf16[8,64,128,128]{3,2,1,0:T(8,128)(2,1)} %bitcast.85, bf16[8,64,128,128]{3,2,1,0:T(8,128)(2,1)} %bitcast.84), kind=kOutput, calls=%fused_computation.11.clone.1 | convolution fusion | flops 2147483648 | bytes 34079232 | tf_op jit(solution)/shard_map/while/body/eval_jaxpr/nkpc,nkqc->npq/dot_general | solution.py:38
  229.9 0.7 dynamic-slice_bitcast_fusion.5
  230.6 7.0 %convolution_convert_fusion.5 = bf16[8,64,16384]{2,1,0:T(8,128)(2,1)S(1)} fusion(bf16[128,16384]{1,0:T(8,128)(2,1)} %get-tuple-element.172, s32[8,64]{1,0:T(8,128)S(1)} %get-tuple-element.151, pred[8,64]{1,0:T(8,128)(4,1)S(1)} %dynamic-slice_bitcast_fusion.6), kind=kOutput, calls=%fused_computation.4.clone.1 | convolution fusion | flops 2156003328 | bytes 20974080 | tf_op jit(solution)/shard_map/while/body/eval_jaxpr/nkm,mx->nkx/dot_general | solution.py:30
  237.6 8.3 %copy.38 = bf16[64,8,128,128]{3,2,1,0:T(8,128)(2,1)} copy(bf16[64,8,128,128]{3,1,2,0:T(8,128)(2,1)S(1)} %bitcast.82) | data formatting | bytes 33554432 | tf_op jit(solution)/shard_map/while
  245.8 6.9 %convolution_convert_fusion.4 = bf16[8,64,16384]{2,1,0:T(8,128)(2,1)S(1)} fusion(bf16[128,16384]{1,0:T(8,128)(2,1)} %get-tuple-element.174, s32[8,64]{1,0:T(8,128)S(1)} %get-tuple-element.150), kind=kOutput, calls=%fused_computation.3.clone.1 | convolution fusion | flops 2155937792 | bytes 20973568 | tf_op jit(solution)/shard_map/while/body/eval_jaxpr/nkm,mx->nkx/dot_general | solution.py:33
  252.8 8.3 %copy.37 = bf16[64,8,128,128]{3,2,1,0:T(8,128)(2,1)} copy(bf16[64,8,128,128]{3,1,2,0:T(8,128)(2,1)S(1)} %bitcast.83) | data formatting | bytes 33554432 | tf_op jit(solution)/shard_map/while
  261.1 13.3 %fusion.30 = f32[4,8,128,128]{3,2,1,0:T(8,128)} fusion(f32[4,8,128,128]{3,2,1,0:T(8,128)} %get-tuple-element.161, s32[]{:T(128)} %get-tuple-element.160, bf16[8,64,128,128]{3,2,1,0:T(8,128)(2,1)} %bitcast.85, bf16[8,64,128,128]{3,2,1,0:T(8,128)(2,1)} %bitcast.84), kind=kOutput, calls=%fused_computation.11.clone.1 | convolution fusion | flops 2147483648 | bytes 34079232 | tf_op jit(solution)/shard_map/while/body/eval_jaxpr/nkpc,nkqc->npq/dot_general | solution.py:38
  274.4 0.7 dynamic-slice_bitcast_fusion.5
  275.1 7.0 %convolution_convert_fusion.5 = bf16[8,64,16384]{2,1,0:T(8,128)(2,1)S(1)} fusion(bf16[128,16384]{1,0:T(8,128)(2,1)} %get-tuple-element.172, s32[8,64]{1,0:T(8,128)S(1)} %get-tuple-element.151, pred[8,64]{1,0:T(8,128)(4,1)S(1)} %dynamic-slice_bitcast_fusion.6), kind=kOutput, calls=%fused_computation.4.clone.1 | convolution fusion | flops 2156003328 | bytes 20974080 | tf_op jit(solution)/shard_map/while/body/eval_jaxpr/nkm,mx->nkx/dot_general | solution.py:30
  282.1 8.3 %copy.38 = bf16[64,8,128,128]{3,2,1,0:T(8,128)(2,1)} copy(bf16[64,8,128,128]{3,1,2,0:T(8,128)(2,1)S(1)} %bitcast.82) | data formatting | bytes 33554432 | tf_op jit(solution)/shard_map/while
  290.4 6.9 %convolution_convert_fusion.4 = bf16[8,64,16384]{2,1,0:T(8,128)(2,1)S(1)} fusion(bf16[128,16384]{1,0:T(8,128)(2,1)} %get-tuple-element.174, s32[8,64]{1,0:T(8,128)S(1)} %get-tuple-element.150), kind=kOutput, calls=%fused_computation.3.clone.1 | convolution fusion | flops 2155937792 | bytes 20973568 | tf_op jit(solution)/shard_map/while/body/eval_jaxpr/nkm,mx->nkx/dot_general | solution.py:33
  297.3 8.3 %copy.37 = bf16[64,8,128,128]{3,2,1,0:T(8,128)(2,1)} copy(bf16[64,8,128,128]{3,1,2,0:T(8,128)(2,1)S(1)} %bitcast.83) | data formatting | bytes 33554432 | tf_op jit(solution)/shard_map/while
  305.6 13.3 %fusion.30 = f32[4,8,128,128]{3,2,1,0:T(8,128)} fusion(f32[4,8,128,128]{3,2,1,0:T(8,128)} %get-tuple-element.161, s32[]{:T(128)} %get-tuple-element.160, bf16[8,64,128,128]{3,2,1,0:T(8,128)(2,1)} %bitcast.85, bf16[8,64,128,128]{3,2,1,0:T(8,128)(2,1)} %bitcast.84), kind=kOutput, calls=%fused_computation.11.clone.1 | convolution fusion | flops 2147483648 | bytes 34079232 | tf_op jit(solution)/shard_map/while/body/eval_jaxpr/nkpc,nkqc->npq/dot_general | solution.py:38
  318.9 0.0 collective-permute-start
  318.9 4.4 %collective-permute-done = f32[32,128,128]{2,1,0:T(8,128)S(1)} collective-permute-done((f32[32,128,128]{2,1,0:T(8,128)}, f32[32,128,128]{2,1,0:T(8,128)S(1)}, u32[]{:S(2)}, u32[]{:S(2)}) %collective-permute-start) | collective-permute-done | bytes 2097184 | tf_op jit(solution)/shard_map/ppermute | solution.py:68
  323.3 0.0 copy-start.1
  323.3 2.0 bitcast_add_fusion
  325.3 1.6 collective-permute-start.1
  326.9 46.2 %collective-permute-done.1 = f32[32,128,128]{2,1,0:T(8,128)S(1)} collective-permute-done((f32[32,128,128]{2,1,0:T(8,128)S(1)}, f32[32,128,128]{2,1,0:T(8,128)S(1)}, u32[]{:S(2)}, u32[]{:S(2)}) %collective-permute-start.1) | collective-permute-done | bytes 2097184 | tf_op jit(solution)/shard_map/ppermute | solution.py:68
  373.1 1.6 add.38
  374.7 3.0 collective-permute-start.2
  377.7 45.6 %collective-permute-done.2 = f32[32,128,128]{2,1,0:T(8,128)} collective-permute-done((f32[32,128,128]{2,1,0:T(8,128)}, f32[32,128,128]{2,1,0:T(8,128)}, u32[]{:S(2)}, u32[]{:S(2)}) %collective-permute-start.2) | collective-permute-done | bytes 2097184 | tf_op jit(solution)/shard_map/ppermute | solution.py:68
  423.3 1.8 dynamic-slice_add_fusion
  425.1 0.0 copy-done.1
  (12 shorter events, 0.1 us)
Async XLA Ops:
  0.0 16.8 %copy-start = (bf16[64,128,128]{2,1,0:T(8,128)(2,1)S(1)}, bf16[64,128,128]{2,1,0:T(8,128)(2,1)}, u32[]{:S(2)}) copy-start(bf16[64,128,128]{2,1,0:T(8,128)(2,1)} %param.9) | copy-start | bytes 6291460
  26.7 5.0 %copy-start.2 = (bf16[64,128,128]{2,1,0:T(8,128)(2,1)S(1)}, bf16[64,128,128]{2,1,0:T(8,128)(2,1)}, u32[]{:S(2)}) copy-start(bf16[64,128,128]{2,1,0:T(8,128)(2,1)} %param.8) | copy-start | bytes 6291460
  26.7 59.3 %all-to-all-start.2 = ((bf16[16,8,128,128]{3,1,2,0:T(8,128)(2,1)}), bf16[16,8,128,128]{3,1,2,0:T(8,128)(2,1)}, u32[]{:S(2)}, u32[]{:S(2)}) async-start(bf16[16,8,128,128]{3,1,2,0:T(8,128)(2,1)} %copy_select_fusion), calls=%async_computation.2 | async-start | bytes 8388608 | tf_op jit(solution)/shard_map/all_to_all | solution.py:56
  41.7 50.0 %copy-start.3 = (s32[32,1]{0,1:T(1,128)S(1)}, s32[32,1]{0,1:T(1,128)}, u32[]{:S(2)}) copy-start(s32[32,1]{0,1:T(1,128)} %param.13) | copy-start | bytes 388
  86.1 54.8 %all-to-all-start.1 = ((bf16[16,8,128,128]{3,1,2,0:T(8,128)(2,1)}), bf16[16,8,128,128]{3,1,2,0:T(8,128)(2,1)}, u32[]{:S(2)}, u32[]{:S(2)}) async-start(bf16[16,8,128,128]{3,1,2,0:T(8,128)(2,1)} %copy_select_fusion.1), calls=%async_computation.1 | async-start | bytes 8388608 | tf_op jit(solution)/shard_map/all_to_all | solution.py:55
  318.9 4.4 %collective-permute-start = (f32[32,128,128]{2,1,0:T(8,128)}, f32[32,128,128]{2,1,0:T(8,128)S(1)}, u32[]{:S(2)}, u32[]{:S(2)}) collective-permute-start(f32[32,128,128]{2,1,0:T(8,128)} %bitcast.88), channel_id=1, source_target_pairs={{0,1},{1,0},{2,3},{3,2},{4,5},{5,4},{6,7},{7,6},{8,9},{9,8},{10,11... | collective-permute-start | bytes 6291464 | tf_op jit(solution)/shard_map/ppermute | solution.py:68
  323.3 101.8 %copy-start.1 = (bf16[64,128,128]{2,1,0:T(8,128)(2,1)S(1)}, bf16[64,128,128]{2,1,0:T(8,128)(2,1)}, u32[]{:S(2)}) copy-start(bf16[64,128,128]{2,1,0:T(8,128)(2,1)} %param.9) | copy-start | bytes 6291460
  325.3 47.8 %collective-permute-start.1 = (f32[32,128,128]{2,1,0:T(8,128)S(1)}, f32[32,128,128]{2,1,0:T(8,128)S(1)}, u32[]{:S(2)}, u32[]{:S(2)}) collective-permute-start(f32[32,128,128]{2,1,0:T(8,128)S(1)} %bitcast_add_fusion), channel_id=1, source_target_pairs={{0,2},{1,3},{2,0},{3,1},{4,6},{5,7},{6,4},{7,5},{8,10},{9,11},{10,... | collective-permute-start | bytes 6291464 | tf_op jit(solution)/shard_map/ppermute | solution.py:68
  374.7 48.6 %collective-permute-start.2 = (f32[32,128,128]{2,1,0:T(8,128)}, f32[32,128,128]{2,1,0:T(8,128)}, u32[]{:S(2)}, u32[]{:S(2)}) collective-permute-start(f32[32,128,128]{2,1,0:T(8,128)} %add.38), channel_id=1, source_target_pairs={{0,4},{1,5},{2,6},{3,7},{4,0},{5,1},{6,2},{7,3},{8,12},{9,13},{10,... | collective-permute-start | bytes 6291464 | tf_op jit(solution)/shard_map/ppermute | solution.py:68
